TPU v7x, 256 devices: a whole 4x4x8 slice. The times are simulated.
256 devices in a mesh: shell: 4 (over z_hi, core), blk: 64 (over z_lo, y, x).
Axes of the slice: x: 4, y: 4, z: 8 (z_hi: 2, z_lo: 4; z = z_hi * 4 + z_lo), core: 2. Of those that a mesh axis runs over, the one named last changes fastest.
Arguments:
- strain_spec: bfloat16 [6, 4, 1024, 2, 1024], P(None, 'shell', 'blk'), may hold values from -6 to 6
- order_map: int32 [1024], replicated, may hold values from 0 to 1023, as said below
- viscosity: float32 [4, 1024, 2048], P('shell', 'blk'), may hold values from 0.2 to 5
- radial_weight: float32 [4], P('shell'), may hold values from 0.3 to 3
Outputs:
- stress_spec: bfloat16 [6, 4, 1024, 2, 1024], P(None, 'shell', 'blk')
- integrated: float32 [6, 1024, 2, 1024], P(None, 'blk', None, 'shell')
Inputs may be any that keep to these rules, and one draw needn't show every extreme that they name: order_map is a permutation of the orders 0 to 1023; the entries 2i and 2i + 1 hold two orders m and 1023 - m, in either order, so each device's 16 slots hold 8 such pairs.
All inputs are finite; a program needn't handle non-finite values.
Results may differ from a plain program's by a relative error of at most 0.014.
Values may be sent and summed in bfloat16 or wider, within the bound.
A program may use at most 128 MiB of HBM per device.

v0:
```python
import math
import jax
import jax.numpy as jnp
from jax import lax
from jax.sharding import PartitionSpec as P

two_power = 1099511627776.0
inverse_power = 1.0 / 1099511627776.0
log_jump = 40.0 * math.log(2.0)


def cycle_geometry(cycle_count):
    cycle_index = jnp.arange(cycle_count // 2, dtype=jnp.float32)
    colatitude = math.pi * (2.0 * cycle_index + 1.0) / (2.0 * cycle_count)
    return (jnp.cos(colatitude), jnp.log(jnp.sin(colatitude)))


def fejer_weights(cycle_count):
    half_count = cycle_count // 2
    cycle_index = jnp.arange(half_count, dtype=jnp.int32)
    wave_number = jnp.arange(1, half_count + 1, dtype=jnp.int32)
    phase_index = wave_number[:, None] * (2 * cycle_index[None, :] + 1) % (2 * cycle_count)
    angles = phase_index.astype(jnp.float32) * (math.pi / cycle_count)
    wave_float = wave_number.astype(jnp.float32)
    divisor = 4.0 * wave_float * wave_float - 1.0
    series = jnp.sum(jnp.cos(angles) / divisor[:, None], axis=0)
    return 2.0 / cycle_count * (1.0 - 2.0 * series)


def legendre_tables(orders, cycle_count, degree_count):
    cosine, log_sine = cycle_geometry(cycle_count)
    order_int = orders[:, None]
    order_float = orders.astype(jnp.float32)[:, None]
    counter = jnp.arange(1, degree_count, dtype=jnp.int32)
    counter_float = counter.astype(jnp.float32)
    factors = jnp.where(
        counter[None, :] <= order_int, jnp.log(1.0 - 0.5 / counter_float)[None, :], 0.0
    )
    log_start = (
        0.5 * jnp.log((2.0 * order_float + 1.0) / (4.0 * math.pi))
        + 0.5 * jnp.sum(factors, axis=1, keepdims=True)
        + order_float * log_sine[None, :]
    )
    even_first = order_int % 2 == 0

    def advance(carry_state, degree):
        previous, latest, log_scale = carry_state
        degree_float = degree.astype(jnp.float32)
        below_float = degree_float - 1.0
        coef_first = jnp.sqrt(
            jnp.maximum(4.0 * degree_float * degree_float - 1.0, 0.0)
            / jnp.maximum(degree_float * degree_float - order_float * order_float, 1.0)
        )
        coef_second = jnp.sqrt(
            jnp.maximum(below_float * below_float - order_float * order_float, 0.0)
            / jnp.maximum(4.0 * below_float * below_float - 1.0, 1.0)
        )
        current = coef_first * (cosine[None, :] * latest - coef_second * previous)
        current = jnp.where(
            degree == order_int + 1,
            jnp.sqrt(2.0 * order_float + 3.0) * cosine[None, :] * latest,
            current,
        )
        current = jnp.where(degree == order_int, 1.0, current)
        current = jnp.where(degree < order_int, 0.0, current)
        result = current * jnp.exp(log_scale)
        too_large = jnp.abs(current) > two_power
        factor = jnp.where(too_large, inverse_power, 1.0)
        next_state = (
            latest * factor,
            current * factor,
            log_scale + jnp.where(too_large, log_jump, 0.0),
        )
        return (next_state, result)

    def pair_step(carry_state, half_degree):
        carry_state, lower_row = advance(carry_state, 2 * half_degree)
        carry_state, upper_row = advance(carry_state, 2 * half_degree + 1)
        even_row = jnp.where(even_first, lower_row, upper_row).astype(jnp.bfloat16)
        odd_row = jnp.where(even_first, upper_row, lower_row).astype(jnp.bfloat16)
        return (carry_state, (even_row, odd_row))

    zero_rows = jnp.zeros((orders.shape[0], cycle_count // 2), jnp.float32)
    initial = (zero_rows, zero_rows, log_start)
    final_state, tables = lax.scan(
        pair_step, initial, jnp.arange(degree_count // 2, dtype=jnp.int32), unroll=32
    )
    return tables


def fourier_table(orders_all, point_count):
    longitudes = jnp.arange(point_count, dtype=jnp.int32)
    phase_index = orders_all[:, None] * longitudes[None, :] % point_count
    angles = phase_index.astype(jnp.float32) * (2.0 * math.pi / point_count)
    return jnp.stack([jnp.cos(angles), -jnp.sin(angles)], axis=1).astype(jnp.bfloat16)


def synthesize(spectra, tables, orders):
    even_first = (orders % 2 == 0)[None, None, :, None, None]
    paired = spectra.reshape(spectra.shape[:-1] + (spectra.shape[-1] // 2, 2))
    even_part = jnp.where(even_first, paired[..., 0], paired[..., 1])
    odd_part = jnp.where(even_first, paired[..., 1], paired[..., 0])
    symmetric = jnp.einsum(
        "csmri,imj->csmrj", even_part, tables[0], preferred_element_type=jnp.float32
    )
    antisymmetric = jnp.einsum(
        "csmri,imj->csmrj", odd_part, tables[1], preferred_element_type=jnp.float32
    )
    north_side = symmetric + antisymmetric
    south_side = symmetric - antisymmetric
    return jnp.concatenate([north_side, jnp.flip(south_side, axis=-1)], axis=-1).astype(
        jnp.bfloat16
    )


def analyze(gridded, tables, orders, weights):
    half_count = gridded.shape[-1] // 2
    north_side = gridded[..., :half_count].astype(jnp.float32)
    south_side = jnp.flip(gridded[..., half_count:], axis=-1).astype(jnp.float32)
    even_side = (weights * (north_side + south_side)).astype(jnp.bfloat16)
    odd_side = (weights * (north_side - south_side)).astype(jnp.bfloat16)
    even_part = jnp.einsum(
        "csmrj,imj->csmri", even_side, tables[0], preferred_element_type=jnp.float32
    )
    odd_part = jnp.einsum(
        "csmrj,imj->csmri", odd_side, tables[1], preferred_element_type=jnp.float32
    )
    even_first = (orders % 2 == 0)[None, None, :, None, None]
    low_side = jnp.where(even_first, even_part, odd_part)
    high_side = jnp.where(even_first, odd_part, even_part)
    stacked = jnp.stack([low_side, high_side], axis=-1)
    return stacked.reshape(stacked.shape[:-2] + (2 * stacked.shape[-2],))


def shards(strain_spec, order_map, viscosity, radial_weight):
    component_count, shell_count, order_count, complex_parts, degree_count = strain_spec.shape
    block_count = lax.axis_size("blk")
    cycle_local = viscosity.shape[1]
    cycle_count = cycle_local * block_count
    point_count = viscosity.shape[2]
    my_orders = lax.dynamic_slice_in_dim(
        order_map, lax.axis_index("blk") * order_count, order_count
    )
    tables = legendre_tables(my_orders, cycle_count, degree_count)
    weights = fejer_weights(cycle_count)
    wave_table = fourier_table(order_map, point_count).reshape(
        block_count, order_count, 2, point_count
    )
    doubling = (
        jnp.where(order_map == 0, 1.0, 2.0).astype(jnp.bfloat16).reshape(block_count, order_count)
    )
    norm_factor = 2.0 * math.pi / point_count
    gridded = synthesize(strain_spec, tables, my_orders)
    item_count = gridded.shape[0]
    pieces = gridded.reshape(item_count, shell_count, order_count, 2, block_count, cycle_local)
    outgoing = pieces.transpose(0, 1, 4, 2, 3, 5).reshape(
        item_count, shell_count, block_count, order_count * 2 * cycle_local
    )
    returns = []
    for component in range(component_count):
        received = lax.all_to_all(
            outgoing[component : component + 1], "blk", split_axis=2, concat_axis=2, tiled=True
        )
        cycle_item_count = received.shape[0]
        blocks = received.reshape(
            cycle_item_count, shell_count, block_count, order_count, 2, cycle_local
        )
        blocks = blocks * doubling[None, None, :, :, None, None]
        grid_field = jnp.einsum(
            "csdxrj,dxrk->csjk", blocks, wave_table, preferred_element_type=jnp.float32
        )
        stress = (viscosity[None] * grid_field).astype(jnp.bfloat16)
        spectra = jnp.einsum(
            "csjk,dxrk->csdxrj", stress, wave_table, preferred_element_type=jnp.float32
        )
        spectra = (spectra * norm_factor).astype(jnp.bfloat16)
        returns.append(
            lax.all_to_all(
                spectra.reshape(
                    cycle_item_count, shell_count, block_count, order_count * 2 * cycle_local
                ),
                "blk",
                split_axis=2,
                concat_axis=2,
                tiled=True,
            )
        )
    returned = jnp.concatenate(returns, axis=0)
    item_count = returned.shape[0]
    pieces = returned.reshape(item_count, shell_count, block_count, order_count, 2, cycle_local)
    coefficient = analyze(
        pieces.transpose(0, 1, 3, 4, 2, 5).reshape(
            item_count, shell_count, order_count, 2, cycle_count
        ),
        tables,
        my_orders,
        weights,
    )
    stress_spec = coefficient.astype(jnp.bfloat16)
    weighted = jnp.sum(coefficient * radial_weight[None, :, None, None, None], axis=1)
    summed = lax.psum(weighted.astype(jnp.bfloat16), "shell").astype(jnp.float32)
    share_size = degree_count // lax.axis_size("shell")
    integrated = lax.dynamic_slice_in_dim(
        summed, lax.axis_index("shell") * share_size, share_size, 3
    )
    return (stress_spec, integrated)


def solution(mesh):
    return jax.shard_map(
        shards,
        mesh=mesh,
        in_specs=(P(None, "shell", "blk", None, None), P(), P("shell", "blk", None), P("shell")),
        out_specs=(P(None, "shell", "blk", None, None), P(None, "blk", None, "shell")),
        check_vma=False,
    )
```

profile of v0, /device:TPU:1, one launch (start us, length us, event | category | flops | bytes accessed | tf_op | source)
XLA Modules:
  0.0 964.2 jit_solution(11079613722453055264)
XLA Ops:
  8.4 453.0 %while.23 = (s32[]{:T(128)}, f32[16,512]{1,0:T(8,128)S(1)}, f32[16,512]{1,0:T(8,128)S(1)}, f32[16,512]{1,0:T(8,128)S(1)}, bf16[16,32,16,512]{3,2,1,0:T(8,128)(2,...) while((s32[]{:T(128)}, f32[16,512]{1,0:T(8,128)S(1)}, ...), condition=%wide.region_2.3_spmd.clone.clone, body=%wide.region_1.2_spmd.clone.clone.sunk | while | flops 11857313 | bytes 9983139 | solution.py:85
  35.5 1.1 bitcast_dynamic-update-slice_fusion.3
  63.8 1.1 bitcast_dynamic-update-slice_fusion.3
  92.2 1.1 bitcast_dynamic-update-slice_fusion.3
  120.5 1.1 bitcast_dynamic-update-slice_fusion.3
  148.8 1.1 bitcast_dynamic-update-slice_fusion.3
  177.1 1.1 bitcast_dynamic-update-slice_fusion.3
  205.4 1.1 bitcast_dynamic-update-slice_fusion.3
  233.7 1.1 bitcast_dynamic-update-slice_fusion.3
  262.0 1.1 bitcast_dynamic-update-slice_fusion.3
  290.3 1.1 bitcast_dynamic-update-slice_fusion.3
  318.6 1.1 bitcast_dynamic-update-slice_fusion.3
  346.9 1.1 bitcast_dynamic-update-slice_fusion.3
  375.2 1.1 bitcast_dynamic-update-slice_fusion.3
  403.5 1.1 bitcast_dynamic-update-slice_fusion.3
  431.8 1.2 bitcast_dynamic-update-slice_fusion.3
  460.2 1.2 bitcast_dynamic-update-slice_fusion.3
  461.4 1.5 copy.242
  462.9 6.0 fusion.637
  468.8 6.5 copy.243
  475.3 6.6 copy.244
  482.1 12.5 %fusion.457 = f32[16,512,6,2]{1,2,3,0:T(8,128)S(1)} fusion(bf16[512,16,512,1]{2,1,0,3:T(8,128)(2,1)} %bitcast.1497, bf16[6,16,2,512]{3,1,2,0:T(8,128)(2,1)S(1)} %get-tuple-element.1382), kind=kOutput, calls=%fused_computation.1301 | convolution fusion | flops 100663296 | bytes 8978432 | tf_op jit(solution)/shard_map/csmri,imj->csmrj/dot_general | solution.py:106
  494.6 9.2 fusion.459
  504.3 1.3 reshape.4640
  506.8 1.3 concatenate.37
  511.9 12.9 %all-to-all-start = ((bf16[64,2,256]{2,1,0:T(2,128)(2,1)}), bf16[64,2,256]{2,1,0:T(2,128)(2,1)S(1)}, u32[]{:S(2)}, u32[]{:S(2)}) async-start(bf16[64,2,256]{2,1,0:T(2,128)(2,1)} %reshape.4644), calls=%async_computation | async-start | bytes 131072 | tf_op jit(solution)/shard_map/all_to_all | solution.py:161
  525.1 1.0 reduce.1
  526.8 6.9 all-to-all-done
  533.7 4.6 all-to-all-start.2
  538.3 37.1 %cosine_convert_fusion = (bf16[64,16,1,2048]{3,0,1,2:T(8,128)(2,1)}, bf16[64,16,1,2048]{3,0,1,2:T(8,128)(2,1)}) fusion(s32[64,16]{0,1:T(8,128)S(1)} %copy.241), kind=kLoop, calls=%fused_computation.1295 | loop fusion | flops 35651584 | bytes 8392704 | tf_op jit(solution)/shard_map/convert.6
  575.5 1.0 reduce.2
  577.2 10.2 %all-to-all-start.4 = ((bf16[64,2,256]{2,1,0:T(2,128)(2,1)}), bf16[64,2,256]{2,1,0:T(2,128)(2,1)S(1)}, u32[]{:S(2)}, u32[]{:S(2)}) async-start(bf16[64,2,256]{2,1,0:T(2,128)(2,1)} %reshape.4652), calls=%async_computation.4 | async-start | bytes 131072 | tf_op jit(solution)/shard_map/all_to_all | solution.py:161
  587.4 7.6 pad_maximum_fusion
  595.2 1.0 reduce.3
  596.9 10.2 %all-to-all-start.6 = ((bf16[64,2,256]{2,1,0:T(2,128)(2,1)}), bf16[64,2,256]{2,1,0:T(2,128)(2,1)S(1)}, u32[]{:S(2)}, u32[]{:S(2)}) async-start(bf16[64,2,256]{2,1,0:T(2,128)(2,1)} %reshape.4656), calls=%async_computation.6 | async-start | bytes 131072 | tf_op jit(solution)/shard_map/all_to_all | solution.py:161
  608.9 7.3 all-to-all-done.6
  616.2 4.6 all-to-all-start.8
  620.8 4.4 fusion.534
  627.1 2.9 all-to-all-done.8
  630.0 7.4 all-to-all-start.10
  639.4 7.3 all-to-all-done.10
  646.9 8.3 fusion.526
  657.1 4.6 all-to-all-start.11
  661.7 8.3 fusion.520
  671.9 10.2 %all-to-all-start.9 = ((bf16[64,2,256]{2,1,0:T(2,128)(2,1)}), bf16[64,2,256]{2,1,0:T(2,128)(2,1)S(1)}, u32[]{:S(2)}, u32[]{:S(2)}) async-start(bf16[64,2,256]{2,1,0:T(2,128)(2,1)} %reshape.4662), calls=%async_computation.9 | async-start | bytes 131072 | tf_op jit(solution)/shard_map/all_to_all | solution.py:178
  682.1 8.3 fusion.514
  692.3 10.4 %all-to-all-start.7 = ((bf16[64,2,256]{2,1,0:T(2,128)(2,1)}), bf16[64,2,256]{2,1,0:T(2,128)(2,1)S(1)}, u32[]{:S(2)}, u32[]{:S(2)}) async-start(bf16[64,2,256]{2,1,0:T(2,128)(2,1)} %reshape.4658), calls=%async_computation.7 | async-start | bytes 131072 | tf_op jit(solution)/shard_map/all_to_all | solution.py:178
  702.7 8.3 fusion.508
  712.8 10.3 %all-to-all-start.5 = ((bf16[64,2,256]{2,1,0:T(2,128)(2,1)}), bf16[64,2,256]{2,1,0:T(2,128)(2,1)S(1)}, u32[]{:S(2)}, u32[]{:S(2)}) async-start(bf16[64,2,256]{2,1,0:T(2,128)(2,1)} %reshape.4654), calls=%async_computation.5 | async-start | bytes 131072 | tf_op jit(solution)/shard_map/all_to_all | solution.py:178
  723.1 8.3 fusion.502
  733.3 10.2 %all-to-all-start.3 = ((bf16[64,2,256]{2,1,0:T(2,128)(2,1)}), bf16[64,2,256]{2,1,0:T(2,128)(2,1)S(1)}, u32[]{:S(2)}, u32[]{:S(2)}) async-start(bf16[64,2,256]{2,1,0:T(2,128)(2,1)} %reshape.4650), calls=%async_computation.3 | async-start | bytes 131072 | tf_op jit(solution)/shard_map/all_to_all | solution.py:178
  743.5 8.3 fusion.496
  753.7 10.2 %all-to-all-start.1 = ((bf16[64,2,256]{2,1,0:T(2,128)(2,1)}), bf16[64,2,256]{2,1,0:T(2,128)(2,1)S(1)}, u32[]{:S(2)}, u32[]{:S(2)}) async-start(bf16[64,2,256]{2,1,0:T(2,128)(2,1)} %reshape.4646), calls=%async_computation.1 | async-start | bytes 131072 | tf_op jit(solution)/shard_map/all_to_all | solution.py:178
  765.0 8.0 all-to-all-done.1
  774.3 2.8 copy.291
  777.2 5.4 reshape.4621
  783.6 12.4 %fusion.461 = f32[16,512,6,2]{1,2,3,0:T(8,128)S(1)} fusion(bf16[512,16,512,1]{2,1,0,3:T(8,128)(2,1)} %bitcast.1493, bf16[6,16,2,512]{3,1,2,0:T(8,128)(2,1)S(1)} %get-tuple-element.1379), kind=kOutput, calls=%fused_computation.1305 | convolution fusion | flops 100663296 | bytes 8978432 | tf_op jit(solution)/shard_map/csmrj,imj->csmri/dot_general | solution.py:122
  796.0 12.5 %fusion.455 = f32[16,512,6,2]{1,2,3,0:T(8,128)S(1)} fusion(bf16[512,16,512,1]{2,1,0,3:T(8,128)(2,1)} %bitcast.1498, bf16[6,16,2,512]{3,1,2,0:T(8,128)(2,1)S(1)} %get-tuple-element.1380), kind=kOutput, calls=%fused_computation.1299 | convolution fusion | flops 100663296 | bytes 8978432 | tf_op jit(solution)/shard_map/csmrj,imj->csmri/dot_general | solution.py:125
  809.0 5.5 copy.300
  814.6 2.2 copy.299
  816.8 2.1 copy.301
  818.9 135.9 %all-reduce.2.cloned.1.call-done = bf16[6,16,2,1024]{1,3,2,0:T(8,128)(2,1)} async-done(((bf16[6,16,2,1024]{1,3,2,0:T(8,128)(2,1)}), bf16[6,16,2,1024]{1,3,2,0:T(8,128)(2,1)}) %all-reduce.2.cloned.1.call-update) | async-done | bytes 393232 | tf_op jit(solution)/shard_map/psum | solution.py:201
  954.8 1.3 dynamic-slice_convert_fusion
  956.1 1.1 copy.302
  (1050 shorter events, 125.9 us)
Async XLA Ops:
  8.4 453.0 %copy-start.2 = (bf16[6,1,16,2,1024]{4,3,2,1,0:T(2,128)(2,1)S(1)}, bf16[6,1,16,2,1024]{4,3,2,1,0:T(2,128)(2,1)}, u32[]{:S(2)}) copy-start(bf16[6,1,16,2,1024]{4,3,2,1,0:T(2,128)(2,1)} %param.6) | copy-start | bytes 1179652
  482.0 12.6 %slice-start = ((s8[8388608]{0:T(1024)(128)(4,1)}), s8[4194304]{0:T(1024)(128)(4,1)S(1)}, s32[]{:S(2)}) async-start(s8[8388608]{0:T(1024)(128)(4,1)} %bitcast.1494), calls=%async_computation.13 | async-start | bytes 8388608
  482.1 12.5 %slice-start.1 = ((s8[8388608]{0:T(1024)(128)(4,1)}), s8[4194304]{0:T(1024)(128)(4,1)S(1)}, s32[]{:S(2)}) async-start(s8[8388608]{0:T(1024)(128)(4,1)} %bitcast.1494), calls=%async_computation.14 | async-start | bytes 8388608
  503.8 21.0 %copy-start.3 = (s32[1024]{0:T(1024)S(1)}, s32[1024]{0:T(1024)}, u32[]{:S(2)}) copy-start(s32[1024]{0:T(1024)} %param.7) | copy-start | bytes 12292
  511.9 21.8 %all-to-all-start = ((bf16[64,2,256]{2,1,0:T(2,128)(2,1)}), bf16[64,2,256]{2,1,0:T(2,128)(2,1)S(1)}, u32[]{:S(2)}, u32[]{:S(2)}) async-start(bf16[64,2,256]{2,1,0:T(2,128)(2,1)} %reshape.4644), calls=%async_computation | async-start | bytes 131072 | tf_op jit(solution)/shard_map/all_to_all | solution.py:161
  533.7 43.6 %all-to-all-start.2 = ((bf16[64,2,256]{2,1,0:T(2,128)(2,1)}), bf16[64,2,256]{2,1,0:T(2,128)(2,1)S(1)}, u32[]{:S(2)}, u32[]{:S(2)}) async-start(bf16[64,2,256]{2,1,0:T(2,128)(2,1)} %reshape.4648), calls=%async_computation.2 | async-start | bytes 131072 | tf_op jit(solution)/shard_map/all_to_all | solution.py:161
  577.2 19.6 %all-to-all-start.4 = ((bf16[64,2,256]{2,1,0:T(2,128)(2,1)}), bf16[64,2,256]{2,1,0:T(2,128)(2,1)S(1)}, u32[]{:S(2)}, u32[]{:S(2)}) async-start(bf16[64,2,256]{2,1,0:T(2,128)(2,1)} %reshape.4652), calls=%async_computation.4 | async-start | bytes 131072 | tf_op jit(solution)/shard_map/all_to_all | solution.py:161
  587.4 59.5 %copy-start = (f32[1,16,2048]{2,1,0:T(8,128)S(1)}, f32[1,16,2048]{2,1,0:T(8,128)}, u32[]{:S(2)}) copy-start(f32[1,16,2048]{2,1,0:T(8,128)} %param.8) | copy-start | bytes 393220
  596.9 19.4 %all-to-all-start.6 = ((bf16[64,2,256]{2,1,0:T(2,128)(2,1)}), bf16[64,2,256]{2,1,0:T(2,128)(2,1)S(1)}, u32[]{:S(2)}, u32[]{:S(2)}) async-start(bf16[64,2,256]{2,1,0:T(2,128)(2,1)} %reshape.4656), calls=%async_computation.6 | async-start | bytes 131072 | tf_op jit(solution)/shard_map/all_to_all | solution.py:161
  616.2 13.8 %all-to-all-start.8 = ((bf16[64,2,256]{2,1,0:T(2,128)(2,1)}), bf16[64,2,256]{2,1,0:T(2,128)(2,1)S(1)}, u32[]{:S(2)}, u32[]{:S(2)}) async-start(bf16[64,2,256]{2,1,0:T(2,128)(2,1)} %reshape.4660), calls=%async_computation.8 | async-start | bytes 131072 | tf_op jit(solution)/shard_map/all_to_all | solution.py:161
  630.0 16.6 %all-to-all-start.10 = ((bf16[64,2,256]{2,1,0:T(2,128)(2,1)}), bf16[64,2,256]{2,1,0:T(2,128)(2,1)S(1)}, u32[]{:S(2)}, u32[]{:S(2)}) async-start(bf16[64,2,256]{2,1,0:T(2,128)(2,1)} %reshape.4664), calls=%async_computation.10 | async-start | bytes 131072 | tf_op jit(solution)/shard_map/all_to_all | solution.py:161
  657.1 14.8 %all-to-all-start.11 = ((bf16[64,2,256]{2,1,0:T(2,128)(2,1)}), bf16[64,2,256]{2,1,0:T(2,128)(2,1)S(1)}, u32[]{:S(2)}, u32[]{:S(2)}) async-start(bf16[64,2,256]{2,1,0:T(2,128)(2,1)} %reshape.4666), calls=%async_computation.11 | async-start | bytes 131072 | tf_op jit(solution)/shard_map/all_to_all | solution.py:178
  671.9 20.4 %all-to-all-start.9 = ((bf16[64,2,256]{2,1,0:T(2,128)(2,1)}), bf16[64,2,256]{2,1,0:T(2,128)(2,1)S(1)}, u32[]{:S(2)}, u32[]{:S(2)}) async-start(bf16[64,2,256]{2,1,0:T(2,128)(2,1)} %reshape.4662), calls=%async_computation.9 | async-start | bytes 131072 | tf_op jit(solution)/shard_map/all_to_all | solution.py:178
  692.3 20.6 %all-to-all-start.7 = ((bf16[64,2,256]{2,1,0:T(2,128)(2,1)}), bf16[64,2,256]{2,1,0:T(2,128)(2,1)S(1)}, u32[]{:S(2)}, u32[]{:S(2)}) async-start(bf16[64,2,256]{2,1,0:T(2,128)(2,1)} %reshape.4658), calls=%async_computation.7 | async-start | bytes 131072 | tf_op jit(solution)/shard_map/all_to_all | solution.py:178
  712.8 20.5 %all-to-all-start.5 = ((bf16[64,2,256]{2,1,0:T(2,128)(2,1)}), bf16[64,2,256]{2,1,0:T(2,128)(2,1)S(1)}, u32[]{:S(2)}, u32[]{:S(2)}) async-start(bf16[64,2,256]{2,1,0:T(2,128)(2,1)} %reshape.4654), calls=%async_computation.5 | async-start | bytes 131072 | tf_op jit(solution)/shard_map/all_to_all | solution.py:178
  733.3 20.4 %all-to-all-start.3 = ((bf16[64,2,256]{2,1,0:T(2,128)(2,1)}), bf16[64,2,256]{2,1,0:T(2,128)(2,1)S(1)}, u32[]{:S(2)}, u32[]{:S(2)}) async-start(bf16[64,2,256]{2,1,0:T(2,128)(2,1)} %reshape.4650), calls=%async_computation.3 | async-start | bytes 131072 | tf_op jit(solution)/shard_map/all_to_all | solution.py:178
  753.7 19.4 %all-to-all-start.1 = ((bf16[64,2,256]{2,1,0:T(2,128)(2,1)}), bf16[64,2,256]{2,1,0:T(2,128)(2,1)S(1)}, u32[]{:S(2)}, u32[]{:S(2)}) async-start(bf16[64,2,256]{2,1,0:T(2,128)(2,1)} %reshape.4646), calls=%async_computation.1 | async-start | bytes 131072 | tf_op jit(solution)/shard_map/all_to_all | solution.py:178
  763.9 190.9 %all-reduce.2.cloned.1.call-start = ((), (), s32[]{:S(2)}) async-start(), calls=%async_computation.12 | async-start | bytes 6291456 | tf_op jit(solution)/shard_map/psum | solution.py:201
  773.4 0.9 copy-start.1
Sparse Core Ops, SparseCore 0:
  814.6 140.1 all-reduce.1
where the time goes:
time: 975 us; the launch traced here: 964 us
  loops' own time  339 us (35%)
  waiting for transfers between devices  168 us (17%)
  other arithmetic  139 us (14%)
  starting transfers between devices  106 us (11%)
  local copies, waits for them, and re-layouts  100 us (10%)
  matrix products  96.4 us (10%)
  between operations  15.6 us (2%)
    another operation x1, loops' own time, legendre_tables(): lax.scan(pair_step, initial, jnp.arange(degree_count // 2, dtype=jnp.int3...  339 us
    psum x1, waiting for transfers between devices, shards(): lax.psum(weighted.astype(jnp.bfloat16), 'shell').astype(jnp.float32)  136 us
    while x496, other arithmetic  56.9 us
    all_to_all x6, starting transfers between devices, shards(): lax.all_to_all(spectra.reshape(cycle_item_count, shell_count, block_count...  55.8 us
    all_to_all x6, starting transfers between devices, shards(): lax.all_to_all(outgoing[component:component + 1], 'blk', split_axis=2, co...  50 us
    dot_general x6, matrix products, shards(): jnp.einsum('csjk,dxrk->csdxrj', stress, wave_table, preferred_element_typ...  49.8 us
    another operation x4, other arithmetic  37.2 us
    all_to_all x6, waiting for transfers between devices, shards(): lax.all_to_all(outgoing[component:component + 1], 'blk', split_axis=2, co...  24.3 us
  transfers between devices with their start and end apart: 13, of which 6 were waited for; matrix products, arithmetic and copies ran while one was open for 12% of the time, Pallas kernels for 0%

commit v1 on v0

--- a/solution.py
+++ b/solution.py
@@ -198,7 +198,9 @@
     )
     stress_spec = coefficient.astype(jnp.bfloat16)
     weighted = jnp.sum(coefficient * radial_weight[None, :, None, None, None], axis=1)
-    summed = lax.psum(weighted.astype(jnp.bfloat16), "shell").astype(jnp.float32)
+    summed = jnp.sum(lax.all_gather(weighted.astype(jnp.bfloat16), "shell"), axis=0).astype(
+        jnp.float32
+    )
     share_size = degree_count // lax.axis_size("shell")
     integrated = lax.dynamic_slice_in_dim(
         summed, lax.axis_index("shell") * share_size, share_size, 3

time: 975 us -> 882 us (0.905)
  waiting for transfers between devices: 168 us -> 66.5 us
    psum x1 -> x0, waiting for transfers between devices: 136 us -> none  [shards(): lax.psum(weighted.astype(jnp.bfloat16), 'shell').astype(jnp.float32)]
    all_gather x0 -> x1, waiting for transfers between devices: none -> 33.7 us  [shards(): lax.all_gather(weighted.astype(jnp.bfloat16), 'shell')]
  transfers between devices with their start and end apart: 13 -> 13, of which waited for: 6 -> 6; matrix products, arithmetic and copies ran while one was open for 12% -> 14% of each run, Pallas kernels for 0% -> 0%
where the time goes in v1:
time: 882 us; the launch traced here: 871 us
  loops' own time  339 us (38%)
  other arithmetic  140 us (16%)
  local copies, waits for them, and re-layouts  107 us (12%)
  starting transfers between devices  106 us (12%)
  matrix products  96.4 us (11%)
  waiting for transfers between devices  66.5 us (8%)
  between operations  15.6 us (2%)
    another operation x1, loops' own time, legendre_tables(): lax.scan(pair_step, initial, jnp.arange(degree_count // 2, dtype=jnp.int3...  339 us
    while x496, other arithmetic  56.9 us
    all_to_all x6, starting transfers between devices, shards(): lax.all_to_all(spectra.reshape(cycle_item_count, shell_count, block_count...  55.8 us
    all_to_all x6, starting transfers between devices, shards(): lax.all_to_all(outgoing[component:component + 1], 'blk', split_axis=2, co...  49.8 us
    dot_general x6, matrix products, shards(): jnp.einsum('csjk,dxrk->csdxrj', stress, wave_table, preferred_element_typ...  49.8 us
    another operation x4, other arithmetic  37.2 us
    all_gather x1, waiting for transfers between devices, shards(): lax.all_gather(weighted.astype(jnp.bfloat16), 'shell')  33.7 us
    all_to_all x6, waiting for transfers between devices, shards(): lax.all_to_all(outgoing[component:component + 1], 'blk', split_axis=2, co...  24.7 us
  transfers between devices with their start and end apart: 13, of which 6 were waited for; matrix products, arithmetic and copies ran while one was open for 14% of the time, Pallas kernels for 0%

profile of v1, /device:TPU:1, one launch (start us, length us, event | category | flops | bytes accessed | tf_op | source)
XLA Modules:
  0.0 870.8 jit_solution(1037555196054859497)
XLA Ops:
  8.4 453.0 %while.23 = (s32[]{:T(128)}, f32[16,512]{1,0:T(8,128)S(1)}, f32[16,512]{1,0:T(8,128)S(1)}, f32[16,512]{1,0:T(8,128)S(1)}, bf16[16,32,16,512]{3,2,1,0:T(8,128)(2,...) while((s32[]{:T(128)}, f32[16,512]{1,0:T(8,128)S(1)}, ...), condition=%wide.region_2.3_spmd.clone.clone, body=%wide.region_1.2_spmd.clone.clone.sunk | while | flops 11857313 | bytes 9983139 | solution.py:85
  35.5 1.1 bitcast_dynamic-update-slice_fusion.3
  63.9 1.1 bitcast_dynamic-update-slice_fusion.3
  92.2 1.1 bitcast_dynamic-update-slice_fusion.3
  120.5 1.1 bitcast_dynamic-update-slice_fusion.3
  148.8 1.1 bitcast_dynamic-update-slice_fusion.3
  177.1 1.1 bitcast_dynamic-update-slice_fusion.3
  205.4 1.1 bitcast_dynamic-update-slice_fusion.3
  233.7 1.1 bitcast_dynamic-update-slice_fusion.3
  262.0 1.1 bitcast_dynamic-update-slice_fusion.3
  290.3 1.1 bitcast_dynamic-update-slice_fusion.3
  318.6 1.1 bitcast_dynamic-update-slice_fusion.3
  346.9 1.1 bitcast_dynamic-update-slice_fusion.3
  375.3 1.1 bitcast_dynamic-update-slice_fusion.3
  403.6 1.1 bitcast_dynamic-update-slice_fusion.3
  431.9 1.2 bitcast_dynamic-update-slice_fusion.3
  460.2 1.1 bitcast_dynamic-update-slice_fusion.3
  461.4 1.5 copy.243
  462.9 6.0 fusion.637
  468.9 6.5 copy.244
  475.4 6.6 copy.245
  482.2 12.5 %fusion.457 = f32[16,512,6,2]{1,2,3,0:T(8,128)S(1)} fusion(bf16[512,16,512,1]{2,1,0,3:T(8,128)(2,1)} %bitcast.1497, bf16[6,16,2,512]{3,1,2,0:T(8,128)(2,1)S(1)} %get-tuple-element.1382), kind=kOutput, calls=%fused_computation.1301 | convolution fusion | flops 100663296 | bytes 8978432 | tf_op jit(solution)/shard_map/csmri,imj->csmrj/dot_general | solution.py:106
  494.7 9.2 %fusion.459 = f32[16,512,6,2]{1,2,3,0:T(8,128)S(1)} fusion(bf16[512,16,512,1]{2,1,0,3:T(8,128)(2,1)S(1)} %bitcast.1496, bf16[6,16,2,512]{3,1,2,0:T(8,128)(2,1)S(1)} %get-tuple-element.1381), kind=kOutput, calls=%fused_computation.1303 | convolution fusion | flops 100663296 | bytes 8978432 | tf_op jit(solution)/shard_map/csmri,imj->csmrj/dot_general | solution.py:103
  504.4 1.3 reshape.4653
  506.9 1.3 concatenate.37
  511.7 12.9 %all-to-all-start = ((bf16[64,2,256]{2,1,0:T(2,128)(2,1)}), bf16[64,2,256]{2,1,0:T(2,128)(2,1)S(1)}, u32[]{:S(2)}, u32[]{:S(2)}) async-start(bf16[64,2,256]{2,1,0:T(2,128)(2,1)} %reshape.4657), calls=%async_computation | async-start | bytes 131072 | tf_op jit(solution)/shard_map/all_to_all | solution.py:161
  524.9 0.9 reduce.2
  526.6 7.0 all-to-all-done
  533.5 4.6 all-to-all-start.2
  538.2 37.1 %cosine_convert_fusion = (bf16[64,16,1,2048]{3,0,1,2:T(8,128)(2,1)}, bf16[64,16,1,2048]{3,0,1,2:T(8,128)(2,1)}) fusion(s32[64,16]{0,1:T(8,128)S(1)} %copy.242), kind=kLoop, calls=%fused_computation.1295 | loop fusion | flops 35651584 | bytes 8392704 | tf_op jit(solution)/shard_map/convert.7
  577.0 10.2 %all-to-all-start.4 = ((bf16[64,2,256]{2,1,0:T(2,128)(2,1)}), bf16[64,2,256]{2,1,0:T(2,128)(2,1)S(1)}, u32[]{:S(2)}, u32[]{:S(2)}) async-start(bf16[64,2,256]{2,1,0:T(2,128)(2,1)} %reshape.4665), calls=%async_computation.4 | async-start | bytes 131072 | tf_op jit(solution)/shard_map/all_to_all | solution.py:161
  587.2 7.6 pad_maximum_fusion
  596.5 10.2 %all-to-all-start.6 = ((bf16[64,2,256]{2,1,0:T(2,128)(2,1)}), bf16[64,2,256]{2,1,0:T(2,128)(2,1)S(1)}, u32[]{:S(2)}, u32[]{:S(2)}) async-start(bf16[64,2,256]{2,1,0:T(2,128)(2,1)} %reshape.4669), calls=%async_computation.6 | async-start | bytes 131072 | tf_op jit(solution)/shard_map/all_to_all | solution.py:161
  608.4 7.4 all-to-all-done.6
  615.9 4.6 all-to-all-start.8
  620.5 4.4 fusion.534
  626.6 3.0 all-to-all-done.8
  629.7 7.3 all-to-all-start.10
  638.9 7.3 all-to-all-done.10
  646.4 8.3 fusion.526
  656.5 4.6 all-to-all-start.11
  661.1 8.3 fusion.520
  671.2 10.2 %all-to-all-start.9 = ((bf16[64,2,256]{2,1,0:T(2,128)(2,1)}), bf16[64,2,256]{2,1,0:T(2,128)(2,1)S(1)}, u32[]{:S(2)}, u32[]{:S(2)}) async-start(bf16[64,2,256]{2,1,0:T(2,128)(2,1)} %reshape.4675), calls=%async_computation.9 | async-start | bytes 131072 | tf_op jit(solution)/shard_map/all_to_all | solution.py:178
  681.4 8.3 fusion.514
  691.4 10.4 %all-to-all-start.7 = ((bf16[64,2,256]{2,1,0:T(2,128)(2,1)}), bf16[64,2,256]{2,1,0:T(2,128)(2,1)S(1)}, u32[]{:S(2)}, u32[]{:S(2)}) async-start(bf16[64,2,256]{2,1,0:T(2,128)(2,1)} %reshape.4671), calls=%async_computation.7 | async-start | bytes 131072 | tf_op jit(solution)/shard_map/all_to_all | solution.py:178
  701.8 8.3 fusion.508
  711.8 10.3 %all-to-all-start.5 = ((bf16[64,2,256]{2,1,0:T(2,128)(2,1)}), bf16[64,2,256]{2,1,0:T(2,128)(2,1)S(1)}, u32[]{:S(2)}, u32[]{:S(2)}) async-start(bf16[64,2,256]{2,1,0:T(2,128)(2,1)} %reshape.4667), calls=%async_computation.5 | async-start | bytes 131072 | tf_op jit(solution)/shard_map/all_to_all | solution.py:178
  722.1 8.3 fusion.502
  732.2 10.2 %all-to-all-start.3 = ((bf16[64,2,256]{2,1,0:T(2,128)(2,1)}), bf16[64,2,256]{2,1,0:T(2,128)(2,1)S(1)}, u32[]{:S(2)}, u32[]{:S(2)}) async-start(bf16[64,2,256]{2,1,0:T(2,128)(2,1)} %reshape.4663), calls=%async_computation.3 | async-start | bytes 131072 | tf_op jit(solution)/shard_map/all_to_all | solution.py:178
  742.4 8.3 fusion.496
  752.4 10.2 %all-to-all-start.1 = ((bf16[64,2,256]{2,1,0:T(2,128)(2,1)}), bf16[64,2,256]{2,1,0:T(2,128)(2,1)S(1)}, u32[]{:S(2)}, u32[]{:S(2)}) async-start(bf16[64,2,256]{2,1,0:T(2,128)(2,1)} %reshape.4659), calls=%async_computation.1 | async-start | bytes 131072 | tf_op jit(solution)/shard_map/all_to_all | solution.py:178
  763.8 8.0 all-to-all-done.1
  773.1 2.8 copy.292
  775.9 5.4 reshape.4634
  782.3 12.4 %fusion.461 = f32[16,512,6,2]{1,2,3,0:T(8,128)S(1)} fusion(bf16[512,16,512,1]{2,1,0,3:T(8,128)(2,1)} %bitcast.1493, bf16[6,16,2,512]{3,1,2,0:T(8,128)(2,1)S(1)} %get-tuple-element.1379), kind=kOutput, calls=%fused_computation.1305 | convolution fusion | flops 100663296 | bytes 8978432 | tf_op jit(solution)/shard_map/csmrj,imj->csmri/dot_general | solution.py:122
  794.7 12.5 %fusion.455 = f32[16,512,6,2]{1,2,3,0:T(8,128)S(1)} fusion(bf16[512,16,512,1]{2,1,0,3:T(8,128)(2,1)} %bitcast.1498, bf16[6,16,2,512]{3,1,2,0:T(8,128)(2,1)S(1)} %get-tuple-element.1380), kind=kOutput, calls=%fused_computation.1299 | convolution fusion | flops 100663296 | bytes 8978432 | tf_op jit(solution)/shard_map/csmrj,imj->csmri/dot_general | solution.py:125
  809.3 5.8 copy.301
  815.1 2.1 copy.302
  817.2 1.8 fusion.535
  819.0 5.8 copy.300
  824.8 2.1 copy.304
  826.9 33.7 %all-gather.2.cloned.1.call-done = bf16[4,6,16,2,1024]{4,2,3,1,0:T(8,128)(2,1)} async-done(((bf16[1,6,16,2,1024]{4,2,3,1,0:T(8,128)(2,1)}), bf16[4,6,16,2,1024]{4,2,3,1,0:T(8,128)(2,1)}) %all-gather.2.cloned.1.call-update) | async-done | bytes 1572880 | tf_op jit(solution)/shard_map/all_gather | solution.py:201
  860.7 1.7 reduce_sum.36
  862.8 1.0 copy.305
  (1055 shorter events, 128.2 us)
Async XLA Ops:
  8.4 453.1 %copy-start.3 = (bf16[6,1,16,2,1024]{4,3,2,1,0:T(2,128)(2,1)S(1)}, bf16[6,1,16,2,1024]{4,3,2,1,0:T(2,128)(2,1)}, u32[]{:S(2)}) copy-start(bf16[6,1,16,2,1024]{4,3,2,1,0:T(2,128)(2,1)} %param.6) | copy-start | bytes 1179652
  482.1 12.6 %slice-start = ((s8[8388608]{0:T(1024)(128)(4,1)}), s8[4194304]{0:T(1024)(128)(4,1)S(1)}, s32[]{:S(2)}) async-start(s8[8388608]{0:T(1024)(128)(4,1)} %bitcast.1494), calls=%async_computation.13 | async-start | bytes 8388608
  482.2 12.5 %slice-start.1 = ((s8[8388608]{0:T(1024)(128)(4,1)}), s8[4194304]{0:T(1024)(128)(4,1)S(1)}, s32[]{:S(2)}) async-start(s8[8388608]{0:T(1024)(128)(4,1)} %bitcast.1494), calls=%async_computation.14 | async-start | bytes 8388608
  503.9 20.8 %copy-start.4 = (s32[1024]{0:T(1024)S(1)}, s32[1024]{0:T(1024)}, u32[]{:S(2)}) copy-start(s32[1024]{0:T(1024)} %param.7) | copy-start | bytes 12292
  511.7 21.8 %all-to-all-start = ((bf16[64,2,256]{2,1,0:T(2,128)(2,1)}), bf16[64,2,256]{2,1,0:T(2,128)(2,1)S(1)}, u32[]{:S(2)}, u32[]{:S(2)}) async-start(bf16[64,2,256]{2,1,0:T(2,128)(2,1)} %reshape.4657), calls=%async_computation | async-start | bytes 131072 | tf_op jit(solution)/shard_map/all_to_all | solution.py:161
  533.5 43.5 %all-to-all-start.2 = ((bf16[64,2,256]{2,1,0:T(2,128)(2,1)}), bf16[64,2,256]{2,1,0:T(2,128)(2,1)S(1)}, u32[]{:S(2)}, u32[]{:S(2)}) async-start(bf16[64,2,256]{2,1,0:T(2,128)(2,1)} %reshape.4661), calls=%async_computation.2 | async-start | bytes 131072 | tf_op jit(solution)/shard_map/all_to_all | solution.py:161
  577.0 19.5 %all-to-all-start.4 = ((bf16[64,2,256]{2,1,0:T(2,128)(2,1)}), bf16[64,2,256]{2,1,0:T(2,128)(2,1)S(1)}, u32[]{:S(2)}, u32[]{:S(2)}) async-start(bf16[64,2,256]{2,1,0:T(2,128)(2,1)} %reshape.4665), calls=%async_computation.4 | async-start | bytes 131072 | tf_op jit(solution)/shard_map/all_to_all | solution.py:161
  587.2 59.2 %copy-start = (f32[1,16,2048]{2,1,0:T(8,128)S(1)}, f32[1,16,2048]{2,1,0:T(8,128)}, u32[]{:S(2)}) copy-start(f32[1,16,2048]{2,1,0:T(8,128)} %param.8) | copy-start | bytes 393220
  596.5 19.4 %all-to-all-start.6 = ((bf16[64,2,256]{2,1,0:T(2,128)(2,1)}), bf16[64,2,256]{2,1,0:T(2,128)(2,1)S(1)}, u32[]{:S(2)}, u32[]{:S(2)}) async-start(bf16[64,2,256]{2,1,0:T(2,128)(2,1)} %reshape.4669), calls=%async_computation.6 | async-start | bytes 131072 | tf_op jit(solution)/shard_map/all_to_all | solution.py:161
  615.9 13.8 %all-to-all-start.8 = ((bf16[64,2,256]{2,1,0:T(2,128)(2,1)}), bf16[64,2,256]{2,1,0:T(2,128)(2,1)S(1)}, u32[]{:S(2)}, u32[]{:S(2)}) async-start(bf16[64,2,256]{2,1,0:T(2,128)(2,1)} %reshape.4673), calls=%async_computation.8 | async-start | bytes 131072 | tf_op jit(solution)/shard_map/all_to_all | solution.py:161
  629.7 16.5 %all-to-all-start.10 = ((bf16[64,2,256]{2,1,0:T(2,128)(2,1)}), bf16[64,2,256]{2,1,0:T(2,128)(2,1)S(1)}, u32[]{:S(2)}, u32[]{:S(2)}) async-start(bf16[64,2,256]{2,1,0:T(2,128)(2,1)} %reshape.4677), calls=%async_computation.10 | async-start | bytes 131072 | tf_op jit(solution)/shard_map/all_to_all | solution.py:161
  656.5 14.7 %all-to-all-start.11 = ((bf16[64,2,256]{2,1,0:T(2,128)(2,1)}), bf16[64,2,256]{2,1,0:T(2,128)(2,1)S(1)}, u32[]{:S(2)}, u32[]{:S(2)}) async-start(bf16[64,2,256]{2,1,0:T(2,128)(2,1)} %reshape.4679), calls=%async_computation.11 | async-start | bytes 131072 | tf_op jit(solution)/shard_map/all_to_all | solution.py:178
  671.2 20.2 %all-to-all-start.9 = ((bf16[64,2,256]{2,1,0:T(2,128)(2,1)}), bf16[64,2,256]{2,1,0:T(2,128)(2,1)S(1)}, u32[]{:S(2)}, u32[]{:S(2)}) async-start(bf16[64,2,256]{2,1,0:T(2,128)(2,1)} %reshape.4675), calls=%async_computation.9 | async-start | bytes 131072 | tf_op jit(solution)/shard_map/all_to_all | solution.py:178
  691.4 20.4 %all-to-all-start.7 = ((bf16[64,2,256]{2,1,0:T(2,128)(2,1)}), bf16[64,2,256]{2,1,0:T(2,128)(2,1)S(1)}, u32[]{:S(2)}, u32[]{:S(2)}) async-start(bf16[64,2,256]{2,1,0:T(2,128)(2,1)} %reshape.4671), calls=%async_computation.7 | async-start | bytes 131072 | tf_op jit(solution)/shard_map/all_to_all | solution.py:178
  711.8 20.3 %all-to-all-start.5 = ((bf16[64,2,256]{2,1,0:T(2,128)(2,1)}), bf16[64,2,256]{2,1,0:T(2,128)(2,1)S(1)}, u32[]{:S(2)}, u32[]{:S(2)}) async-start(bf16[64,2,256]{2,1,0:T(2,128)(2,1)} %reshape.4667), calls=%async_computation.5 | async-start | bytes 131072 | tf_op jit(solution)/shard_map/all_to_all | solution.py:178
  732.2 20.2 %all-to-all-start.3 = ((bf16[64,2,256]{2,1,0:T(2,128)(2,1)}), bf16[64,2,256]{2,1,0:T(2,128)(2,1)S(1)}, u32[]{:S(2)}, u32[]{:S(2)}) async-start(bf16[64,2,256]{2,1,0:T(2,128)(2,1)} %reshape.4663), calls=%async_computation.3 | async-start | bytes 131072 | tf_op jit(solution)/shard_map/all_to_all | solution.py:178
  752.4 19.4 %all-to-all-start.1 = ((bf16[64,2,256]{2,1,0:T(2,128)(2,1)}), bf16[64,2,256]{2,1,0:T(2,128)(2,1)S(1)}, u32[]{:S(2)}, u32[]{:S(2)}) async-start(bf16[64,2,256]{2,1,0:T(2,128)(2,1)} %reshape.4659), calls=%async_computation.1 | async-start | bytes 131072 | tf_op jit(solution)/shard_map/all_to_all | solution.py:178
  762.6 98.1 %all-gather.2.cloned.1.call-start = ((), (), s32[]{:S(2)}) async-start(), calls=%async_computation.12 | async-start | bytes 1966080 | tf_op jit(solution)/shard_map/all_gather | solution.py:201
  772.2 0.9 copy-start.2
  807.7 0.7 copy-start.1
Sparse Core Ops, SparseCore 0:
  817.3 43.3 all-gather.1
